TPU v7x, 32 devices: a whole 2x2x4 slice. The times are simulated.
32 devices in a mesh: tile: 8 (over z, x), member: 4 (over y, core).
Axes of the slice: x: 2, y: 2, z: 4, core: 2. Of those that a mesh axis runs over, the one named last changes fastest.
Arguments:
- noise: float32 [4, 512, 512], P('member', 'tile'), as said below
- observed: bfloat16 [2, 6, 512, 512], P(None, None, 'tile'), may hold values from -6 to 6
- row_shift: int32 [512, 512], P('tile'), may hold values from -4 to 4
- col_shift: int32 [512, 512], P('tile'), may hold values from -4 to 4
- rain_mask: int32 [64, 4], P('tile'), may hold values 0 or 1
- autocorr: float32 [2, 6], replicated, may hold values from 0.09 to 0.97, as said below
- level_scale: float32 [6], replicated, may hold values from 0.2 to 2
Outputs:
- forecast: bfloat16 [4, 512, 512], P('member', 'tile')
- ensemble_mean: float32 [512, 512], P('tile')
Inputs may be any that keep to these rules, and one draw needn't show every extreme that they name: row_shift, along with col_shift, is bounded by 4 in magnitude. `autocorr`: row 1 of each level lies between the square of row 0 and row 0. `noise`: finite values.
All inputs are finite; a program needn't handle non-finite values. No bound on the sum of `rain_mask` on one device may be relied on, other than what follows from the above.
Results may differ from a plain program's by a relative error of at most 0.01.
Values may be sent and summed in bfloat16 or wider, within the bound.
A program may use at most 64 MiB of HBM per device.

v0:
```python
import functools
import math

import jax
import jax.numpy as jnp
import numpy as np
from jax import lax
from jax.experimental import pallas as pl
from jax.experimental.pallas import tpu as pltpu
from jax.sharding import PartitionSpec as P

LEVELS = 6
HALO = 4
PAD = 8
F32 = jnp.float32
BF16 = jnp.bfloat16


def real_basis(length):
    half = length // 2
    positions = np.arange(length)
    angles = 2.0 * math.pi * (np.outer(np.arange(half), positions) % length) / length
    cosines = np.cos(angles) * math.sqrt(2.0 / length)
    sines = np.sin(angles) * math.sqrt(2.0 / length)
    cosines[0] = 1.0 / math.sqrt(length)
    sines[0] = (1.0 - 2.0 * (positions % 2)) / math.sqrt(length)
    return np.concatenate([cosines, sines], axis=0)


def band_table(height, width):
    freq_y = np.arange(height // 2 + PAD)[:, None] / height
    freq_x = np.arange(width // 2 + 128)[None, :] / width
    longest = max(height, width)
    log_radius = np.log(longest * np.sqrt(freq_y * freq_y + freq_x * freq_x) + 1.0)
    spacing = math.log(longest / 2.0) / (LEVELS - 1)
    offsets = log_radius[None] - spacing * np.arange(LEVELS)[:, None, None]
    bumps = np.exp(-(offsets * offsets) / (2.0 * (0.6 * spacing) ** 2))
    return bumps / np.sum(bumps, axis=0, keepdims=True)


def chunk_of(rows):
    return rows // 2 if rows % 32 == 0 else rows


def split(value):
    high = value.astype(BF16)
    return high, (value - high.astype(F32)).astype(BF16)


def dot(a, b):
    return jnp.dot(a, b, preferred_element_type=F32)


def coefficients(ac, scale, k, width):
    g1 = jnp.full((1, width), ac[0, k], F32)
    g2 = jnp.full((1, width), ac[1, k], F32)
    s = jnp.full((1, width), scale[k], F32)
    den = 1.0 - g1 * g1
    one = g1 * (1.0 - g2) / den
    two = (g2 - g1 * g1) / den
    innovation = jnp.sqrt(1.0 - one * g1 - two * g2)
    return s * one, s * two, s * innovation


def write_out(fc, mean, fc_hbm, mean_hbm, sem):
    copies = [pltpu.make_async_copy(a, b, sem.at[i]) for i, (a, b) in enumerate([(fc, fc_hbm), (mean, mean_hbm)])]
    for copy in copies:
        copy.start()
    for copy in copies:
        copy.wait()


def kernel(
    tiles, pair, members,
    noise_hbm, obs_hbm, row_hbm, col_hbm, rain, ac, scale, ty_hbm, tx_hbm, txt_hbm, tyt_hbm, band_hbm,
    fc_out, mean,
    noise, obs, row, col, ty, tx, txt, txtl, rows_t, band,
    xg, pad, shifted, steady, mask, spec, gain, arrived,
    load_sem, send_sem, cross_sem, recv_sem, halo_send, halo_recv, mem_send, mem_recv,
):
    fc = fc_out.at[0]
    rows, width = noise.shape
    height = rows * tiles
    hy, hx = height // 2, width // 2
    depth = tiles // pair
    size = chunk_of(rows)
    chunks = rows // size
    t = lax.axis_index("tile")
    m = lax.axis_index("member")
    z = t // pair
    x = t % pair

    sources = [
        (noise_hbm.at[0], noise), (txt_hbm.at[0], txt), (txt_hbm.at[1], txtl), (obs_hbm, obs), (row_hbm, row), (col_hbm, col),
        (ty_hbm, ty), (band_hbm, band),
        (tyt_hbm.at[:, pl.ds(pl.multiple_of(t * rows, rows), rows), :], rows_t), (tx_hbm, tx),
    ]
    loads = [pltpu.make_async_copy(a, b, load_sem.at[i]) for i, (a, b) in enumerate(sources)]
    for load in loads:
        load.start()

    barrier = pltpu.get_barrier_semaphore()
    greeted = 0
    near = sorted({pair * d for d in range(1, depth)} | {1})
    for step in [sign * d for d in near for sign in (-1, 1)]:
        there = jnp.logical_and(t + step >= 0, t + step < tiles)
        greeted = greeted + there.astype(jnp.int32)

        @pl.when(there)
        def _():
            pl.semaphore_signal(barrier, inc=1, device_id={"tile": t + step}, device_id_type=pl.DeviceIdType.MESH)

    for d in range(1, members):
        pl.semaphore_signal(
            barrier, inc=1, device_id={"member": (m + d) % members}, device_id_type=pl.DeviceIdType.MESH
        )

    for load in loads[:3]:
        load.wait()
    own = pl.multiple_of(t * rows, rows)
    n_hi, n_lo = split(noise[...])
    first = dot(jnp.concatenate([n_hi, n_lo], axis=0), txt[...])
    xg[pl.ds(own, rows), :] = (first[:rows] + first[rows:] + dot(n_hi, txtl[...])).astype(BF16)
    pl.semaphore_wait(barrier, greeted + members - 1)

    def part(block, c):
        return xg.at[pl.ds(pl.multiple_of(block * rows + c * size, size), size), :]

    def along(up, d, c):
        mine = part(t, c)
        return pltpu.make_async_remote_copy(
            src_ref=mine, dst_ref=mine, send_sem=send_sem.at[up, d, c], recv_sem=recv_sem.at[t, c],
            device_id={"tile": t + pair * (d if up else -d)}, device_id_type=pl.DeviceIdType.MESH,
        )

    def across(zb, c):
        block = part(zb * pair + x, c)
        return pltpu.make_async_remote_copy(
            src_ref=block, dst_ref=block, send_sem=cross_sem.at[zb, c], recv_sem=recv_sem.at[zb * pair + x, c],
            device_id={"tile": z * pair + 1 - x}, device_id_type=pl.DeviceIdType.MESH,
        )

    def arrival(block, c):
        pltpu.make_async_copy(part(block, c), part(block, c), recv_sem.at[block, c]).wait()

    def both_ways(d, act):
        @pl.when(z + d < depth)
        def _():
            act(1)

        @pl.when(z - d >= 0)
        def _():
            act(0)

    for c in range(chunks):
        if pair > 1:
            across(z, c).start()
        for d in range(depth - 1, 0, -1):
            both_ways(d, lambda up: along(up, d, c).start())

    def relay(s):
        def take(up, c):
            zb = z + s if up else z - s
            arrival(zb * pair + x, c)
            if pair > 1:
                across(zb, c).start()

        for c in range(chunks):
            both_ways(s, lambda up: take(up, c))

    loads[3].wait()
    coef = [coefficients(ac, scale, k, width) for k in range(LEVELS)]
    for g in range(rows // 16):
        span = pl.ds(16 * g, 16)
        total = jnp.zeros((16, width), F32)
        for k in range(LEVELS):
            total += coef[k][0] * obs[0, k, span, :].astype(F32) + coef[k][1] * obs[1, k, span, :].astype(F32)
        pad[pl.ds(PAD + 16 * g, 16), :] = total
    for i in range(rows // 8):
        for j in range(width // 128):
            mask[8 * i : 8 * i + 8, 128 * j : 128 * j + 128] = jnp.full((8, 128), rain[j, i].astype(F32), F32)

    after = pltpu.make_async_remote_copy(
        src_ref=pad.at[pl.ds(rows, PAD), :], dst_ref=pad.at[pl.ds(0, PAD), :],
        send_sem=halo_send.at[0], recv_sem=halo_recv.at[0],
        device_id={"tile": t + 1}, device_id_type=pl.DeviceIdType.MESH,
    )
    before = pltpu.make_async_remote_copy(
        src_ref=pad.at[pl.ds(PAD, PAD), :], dst_ref=pad.at[pl.ds(rows + PAD, PAD), :],
        send_sem=halo_send.at[1], recv_sem=halo_recv.at[1],
        device_id={"tile": t - 1}, device_id_type=pl.DeviceIdType.MESH,
    )

    @pl.when(t < tiles - 1)
    def _():
        after.start()

    @pl.when(t == tiles - 1)
    def _():
        pad[rows + PAD :, :] = jnp.zeros((PAD, width), F32)

    @pl.when(t > 0)
    def _():
        before.start()

    @pl.when(t == 0)
    def _():
        pad[:PAD, :] = jnp.zeros((PAD, width), F32)

    def shift_columns():
        lane = lax.broadcasted_iota(jnp.int32, (rows + 2 * PAD, width), 1)
        value = pad[...]
        for dx in range(-HALO, HALO + 1):
            moved = pltpu.roll(value, dx % width, 1) if dx else value
            if dx > 0:
                moved = jnp.where(lane >= dx, moved, 0.0)
            if dx < 0:
                moved = jnp.where(lane < width + dx, moved, 0.0)
            shifted[dx + HALO] = moved

    def gather_rows(start, stop):
        for g in range(start, stop):
            span = pl.ds(8 * g, 8)
            code = row[span, :] * (2 * HALO + 1) + col[span, :]
            total = jnp.zeros((8, width), F32)
            for dy in range(-HALO, HALO + 1):
                for dx in range(-HALO, HALO + 1):
                    total = jnp.where(
                        code == dy * (2 * HALO + 1) + dx,
                        shifted[dx + HALO, 8 * g + PAD - dy : 8 * g + PAD - dy + 8, :],
                        total,
                    )
            steady[span, :] = total

    for s in range(1, depth):
        relay(s)

    @pl.when(t > 0)
    def _():
        after.wait_recv()

    @pl.when(t < tiles - 1)
    def _():
        before.wait_recv()

    groups = rows // 8
    shift_columns()
    loads[4].wait()
    loads[5].wait()
    steps = max(depth - 1, 1)
    for s in range(1, depth):
        gather_rows(groups * (s - 1) // steps, groups * s // steps)
    if depth == 1:
        gather_rows(0, groups)
    for load in loads[6:]:
        load.wait()
    if pair > 1:
        for zb in range(depth):
            for c in range(chunks):
                arrival(zb * pair + 1 - x, c)

    spec[...] = dot(ty[...], xg[...])
    strip = 16
    lane = lax.broadcasted_iota(jnp.int32, (strip, hx), 1)
    lane_one = lax.broadcasted_iota(jnp.int32, (strip, 128), 1)
    sub = lax.broadcasted_iota(jnp.int32, (strip, hx), 0)

    def fold(value):
        return value[:8] + value[8:]

    def powers(i, sums):
        r = pl.multiple_of(i * strip, strip)
        top = pl.ds(r, strip)
        low = pl.ds(hy + r, strip)
        cc, cs = spec[top, :hx], spec[top, hx:]
        sc, ss = spec[low, :hx], spec[low, hx:]
        cc, cs, sc, ss = cc * cc, cs * cs, sc * sc, ss * ss
        inner = sub + r > 0
        sc = jnp.where(inner, sc, 0.0)
        ss = jnp.where(inner, ss, 0.0)
        right = cs + ss
        energy = cc + sc + jnp.where(lane > 0, right, 0.0)
        edge = jnp.where(lane_one == 0, right[:, :128], 0.0)
        out = []
        for k in range(LEVELS):
            w = band[k, top, :hx].astype(F32)
            e = band[k, top, hx:].astype(F32)
            out.append((sums[2 * k] + fold(w * w * energy)))
            out.append((sums[2 * k + 1] + fold(e * e * edge)))
        return tuple(out)

    sc, ss = spec[hy : hy + 8, :hx], spec[hy : hy + 8, hx:]
    sc, ss = sc * sc, ss * ss
    first_row = sub[:8] == 0
    bottom = jnp.where(first_row, sc + jnp.where(lane[:8] > 0, ss, 0.0), 0.0)
    corner = jnp.where(jnp.logical_and(first_row[:, :128], lane_one[:8] == 0), ss[:, :128], 0.0)
    sums = []
    for k in range(LEVELS):
        w = band[k, hy:, :hx].astype(F32)
        e = band[k, hy:, hx:].astype(F32)
        sums += [w * w * bottom, e * e * corner]
    sums = lax.fori_loop(0, hy // strip, powers, tuple(sums), unroll=2)
    levels = []
    for k in range(LEVELS):
        both = jnp.concatenate([sums[2 * k], sums[2 * k + 1]], axis=1)
        power = jnp.sum(jnp.sum(both, axis=0, keepdims=True), axis=1, keepdims=True) / float(height * width)
        levels.append(coef[k][2][:, :1] / jnp.sqrt(power + 1e-06))
    level = [jnp.broadcast_to(v, (1, hx + 128)) for v in levels]

    last = sum(level[k] * band[k, hy:, :].astype(F32) for k in range(LEVELS))[:1]

    def apply(i, carry):
        r = pl.multiple_of(i * strip, strip)
        top = pl.ds(r, strip)
        low = pl.ds(hy + r, strip)
        a = level[0] * band[0, top, :].astype(F32)
        for k in range(1, LEVELS):
            a += level[k] * band[k, top, :].astype(F32)

        def right_of(v):
            begin = jnp.where(lane_one == 0, v[:, hx:], v[:, :128])
            return jnp.concatenate([begin, v[:, 128:hx]], axis=1) if hx > 128 else begin

        gain[top, :hx] = (a[:, :hx] * spec[top, :hx]).astype(BF16)
        gain[top, hx:] = (right_of(a) * spec[top, hx:]).astype(BF16)
        wide = lax.broadcasted_iota(jnp.int32, (strip, hx + 128), 0) + r
        b = jnp.where(wide == 0, last, a)
        gain[low, :hx] = (b[:, :hx] * spec[low, :hx]).astype(BF16)
        gain[low, hx:] = (right_of(b) * spec[low, hx:]).astype(BF16)
        return carry

    lax.fori_loop(0, hy // strip, apply, 0, unroll=2)

    back = dot(jnp.concatenate([rows_t[0], rows_t[1]], axis=0), gain[...])
    b_hi, b_lo = split(back[:rows] + back[rows:])
    field = dot(jnp.concatenate([b_hi, b_lo], axis=0), tx[...])
    raw = (steady[...] + (field[:rows] + field[rows:])) * mask[...]
    mean[...] = raw
    fc[...] = raw.astype(BF16)

    sends = [
        pltpu.make_async_remote_copy(
            src_ref=fc, dst_ref=arrived.at[d - 1], send_sem=mem_send.at[d - 1], recv_sem=mem_recv.at[d - 1],
            device_id={"member": (m + d) % members}, device_id_type=pl.DeviceIdType.MESH,
        )
        for d in range(1, members)
    ]
    for send in sends:
        send.start()

    for c in range(chunks):
        for d in range(1, depth):
            both_ways(d, lambda up: along(up, d, c).wait_send())
        if pair > 1:
            for zb in range(depth):
                across(zb, c).wait_send()

    @pl.when(t < tiles - 1)
    def _():
        after.wait_send()

    @pl.when(t > 0)
    def _():
        before.wait_send()

    total = mean[...]
    for d in range(1, members):
        sends[d - 1].wait_recv()
        total += arrived[d - 1].astype(F32)
    mean[...] = total * (1.0 / members)
    for send in sends:
        send.wait_send()


def shards(tables, tiles, members, noise, observed, row_shift, col_shift, rain_mask, autocorr, level_scale):
    _, rows, width = noise.shape
    height = rows * tiles
    pair = 2 if tiles % 2 == 0 else 1
    depth, chunks = tiles // pair, rows // chunk_of(rows)
    any_space = pl.BlockSpec(memory_space=pl.ANY)
    smem = pl.BlockSpec(memory_space=pltpu.SMEM)
    dma = pltpu.SemaphoreType.DMA
    peers = max(members - 1, 1)
    fields = pl.pallas_call(
        functools.partial(kernel, tiles, pair, members),
        out_shape=(pltpu.VMEM((1, rows, width), BF16), pltpu.VMEM((rows, width), F32)),
        in_specs=[any_space] * 4 + [smem] * 3 + [any_space] * 5,
        out_specs=(pl.BlockSpec(memory_space=pltpu.VMEM),) * 2,
        scratch_shapes=[
            pltpu.VMEM((rows, width), F32),
            pltpu.VMEM(observed.shape, BF16),
            pltpu.VMEM((rows, width), jnp.int32),
            pltpu.VMEM((rows, width), jnp.int32),
            pltpu.VMEM((height, height), BF16),
            pltpu.VMEM((width, width), BF16),
            pltpu.VMEM((width, width), BF16),
            pltpu.VMEM((width, width), BF16),
            pltpu.VMEM((2, rows, height), BF16),
            pltpu.VMEM(tables[-1].shape, BF16),
            pltpu.VMEM((height, width), BF16),
            pltpu.VMEM((rows + 2 * PAD, width), F32),
            pltpu.VMEM((2 * HALO + 1, rows + 2 * PAD, width), F32),
            pltpu.VMEM((rows, width), F32),
            pltpu.VMEM((rows, width), F32),
            pltpu.VMEM((height, width), F32),
            pltpu.VMEM((height, width), BF16),
            pltpu.VMEM((peers, rows, width), BF16),
            dma((10,)),
            dma((2, depth, chunks)),
            dma((depth, chunks)),
            dma((tiles, chunks)),
            dma((2,)),
            dma((2,)),
            dma((peers,)),
            dma((peers,)),
        ],
        compiler_params=pltpu.CompilerParams(
            collective_id=0, has_side_effects=True, vmem_limit_bytes=67043328 - 4 * 64 * 1024
        ),
        name="nowcast",
    )(noise, observed, row_shift, col_shift, rain_mask.T, autocorr, level_scale, *tables)
    return pl.pallas_call(
        write_out,
        out_shape=(
            jax.ShapeDtypeStruct((1, rows, width), BF16),
            jax.ShapeDtypeStruct((rows, width), F32),
        ),
        in_specs=[pl.BlockSpec(memory_space=pltpu.VMEM)] * 2,
        out_specs=(any_space, any_space),
        scratch_shapes=[dma((2,))],
        compiler_params=pltpu.CompilerParams(vmem_limit_bytes=1024 * 1024),
        name="write_out",
    )(*fields)


def solution(mesh):
    tiles, members = mesh.shape["tile"], mesh.shape["member"]
    in_specs = (
        P("member", "tile", None),
        P(None, None, "tile", None),
        P("tile", None),
        P("tile", None),
        P("tile", None),
        P(),
        P(),
    )
    out_specs = (P("member", "tile", None), P("tile", None))

    def program(noise, observed, *rest):
        height, width = noise.shape[1:]

        def halves(table):
            high = table.astype(jnp.bfloat16)
            return high, (table - high.astype(np.float64)).astype(jnp.bfloat16)

        basis_y, basis_x = real_basis(height), real_basis(width)
        tables = (
            basis_y.astype(jnp.bfloat16),
            basis_x.astype(jnp.bfloat16),
            np.stack(halves(np.ascontiguousarray(basis_x.T))),
            np.stack(halves(np.ascontiguousarray(basis_y.T))),
            band_table(height, width).astype(jnp.bfloat16),
        )
        body = functools.partial(shards, tables, tiles, members)
        return jax.shard_map(body, mesh=mesh, in_specs=in_specs, out_specs=out_specs, check_vma=False)(
            noise, observed, *rest
        )

    return program
```

profile of v0, /device:TPU:1, one launch (start us, length us, event | category | flops | bytes accessed | tf_op | source)
XLA Modules:
  0.0 23.9 jit_solution(15704756612031190435)
XLA Ops:
  0.6 22.6 %nowcast.1 = (bf16[1,64,512]{2,1,0:T(8,128)(2,1)S(1)}, f32[64,512]{1,0:T(8,128)S(1)}) custom-call(f32[1,64,512]{2,1,0:T(8,128)} %noise_hbm.1, bf16[2,6,64,512]{3,2,1,0:T(8,128)(2,1)} %obs_hbm.1, s32[64,512]{1,0:T(8,128)} %row_hbm.1, s32[64,512]{1,0:T(8,128)} %col_hbm.1, s32[4,8]{1,0:T(4,128)} %bitcast.1, f32[2,6]{1,0:T(2,128)} %ac.1, f32[6]{0:T(128)} %scale.1, ...), custom_call_target="tpu_custom_call" | custom-call | tf_op jit(solution)/shard_map/nowcast/pallas_call | solution.py:384
  23.2 0.7 %write_out.1 = (bf16[1,64,512]{2,1,0:T(8,128)(2,1)}, f32[64,512]{1,0:T(8,128)}) custom-call(bf16[1,64,512]{2,1,0:T(8,128)(2,1)S(1)} %get-tuple-element.4.fc, f32[64,512]{1,0:T(8,128)S(1)} %get-tuple-element.5.mean), custom_call_target="tpu_custom_call" | custom-call | tf_op jit(solution)/shard_map/write_out/pallas_call | solution.py:422
where the time goes:
time: 24.1 us; the launch traced here: 23.9 us
  Pallas kernels  23.3 us (97%)
  between operations  0.64 us (3%)
    pallas_call x1, Pallas kernels, shards(): pl.pallas_call(functools.partial(kernel, tiles, pair, members), out_shape...  22.6 us
    pallas_call x1, Pallas kernels, shards(): pl.pallas_call(write_out, out_shape=(jax.ShapeDtypeStruct((1, rows, width...  0.7 us

commit v1 on v0

--- a/solution.py
+++ b/solution.py
@@ -72,10 +72,10 @@
 
 def kernel(
     tiles, pair, members,
-    noise_hbm, obs_hbm, row_hbm, col_hbm, rain, ac, scale, ty_hbm, tx_hbm, txt_hbm, tyt_hbm, band_hbm,
+    noise_hbm, obs_hbm, row_hbm, col_hbm, rain_hbm, ac_hbm, scale_hbm, ty_hbm, tx_hbm, txt_hbm, tyt_hbm, band_hbm,
     fc_out, mean,
     noise, obs, row, col, ty, tx, txt, txtl, rows_t, band,
-    xg, pad, shifted, steady, mask, spec, gain, arrived,
+    xg, pad, shifted, steady, mask, spec, gain, arrived, rain, ac, scale,
     load_sem, send_sem, cross_sem, recv_sem, halo_send, halo_recv, mem_send, mem_recv,
 ):
     fc = fc_out.at[0]
@@ -91,12 +91,13 @@
     x = t % pair
 
     sources = [
-        (noise_hbm.at[0], noise), (txt_hbm.at[0], txt), (txt_hbm.at[1], txtl), (obs_hbm, obs), (row_hbm, row), (col_hbm, col),
+        (noise_hbm.at[0], noise), (txt_hbm.at[0], txt), (txt_hbm.at[1], txtl),
+        (rain_hbm, rain), (ac_hbm, ac), (scale_hbm, scale), (obs_hbm, obs), (row_hbm, row), (col_hbm, col),
         (ty_hbm, ty), (band_hbm, band),
         (tyt_hbm.at[:, pl.ds(pl.multiple_of(t * rows, rows), rows), :], rows_t), (tx_hbm, tx),
     ]
     loads = [pltpu.make_async_copy(a, b, load_sem.at[i]) for i, (a, b) in enumerate(sources)]
-    for load in loads:
+    for load in loads[:3]:
         load.start()
 
     barrier = pltpu.get_barrier_semaphore()
@@ -115,6 +116,8 @@
             barrier, inc=1, device_id={"member": (m + d) % members}, device_id_type=pl.DeviceIdType.MESH
         )
 
+    for load in loads[3:]:
+        load.start()
     for load in loads[:3]:
         load.wait()
     own = pl.multiple_of(t * rows, rows)
@@ -168,7 +171,8 @@
         for c in range(chunks):
             both_ways(s, lambda up: take(up, c))
 
-    loads[3].wait()
+    for load in loads[3:7]:
+        load.wait()
     coef = [coefficients(ac, scale, k, width) for k in range(LEVELS)]
     for g in range(rows // 16):
         span = pl.ds(16 * g, 16)
@@ -245,14 +249,14 @@
 
     groups = rows // 8
     shift_columns()
-    loads[4].wait()
-    loads[5].wait()
+    loads[7].wait()
+    loads[8].wait()
     steps = max(depth - 1, 1)
     for s in range(1, depth):
         gather_rows(groups * (s - 1) // steps, groups * s // steps)
     if depth == 1:
         gather_rows(0, groups)
-    for load in loads[6:]:
+    for load in loads[9:]:
         load.wait()
     if pair > 1:
         for zb in range(depth):
@@ -378,13 +382,12 @@
     pair = 2 if tiles % 2 == 0 else 1
     depth, chunks = tiles // pair, rows // chunk_of(rows)
     any_space = pl.BlockSpec(memory_space=pl.ANY)
-    smem = pl.BlockSpec(memory_space=pltpu.SMEM)
     dma = pltpu.SemaphoreType.DMA
     peers = max(members - 1, 1)
     fields = pl.pallas_call(
         functools.partial(kernel, tiles, pair, members),
         out_shape=(pltpu.VMEM((1, rows, width), BF16), pltpu.VMEM((rows, width), F32)),
-        in_specs=[any_space] * 4 + [smem] * 3 + [any_space] * 5,
+        in_specs=[any_space] * 12,
         out_specs=(pl.BlockSpec(memory_space=pltpu.VMEM),) * 2,
         scratch_shapes=[
             pltpu.VMEM((rows, width), F32),
@@ -405,7 +408,10 @@
             pltpu.VMEM((height, width), F32),
             pltpu.VMEM((height, width), BF16),
             pltpu.VMEM((peers, rows, width), BF16),
-            dma((10,)),
+            pltpu.SMEM(rain_mask.shape[::-1], jnp.int32),
+            pltpu.SMEM(autocorr.shape, F32),
+            pltpu.SMEM(level_scale.shape, F32),
+            dma((13,)),
             dma((2, depth, chunks)),
             dma((depth, chunks)),
             dma((tiles, chunks)),

time: 24.1 us -> 23.4 us (0.971)
  Pallas kernels: 23.3 us -> 22.6 us
    pallas_call x1, Pallas kernels: 22.6 us -> 21.9 us  [shards(): pl.pallas_call(functools.partial(kernel, tiles, pair, members), out_shape...]
where the time goes in v1:
time: 23.4 us; the launch traced here: 23.2 us
  Pallas kernels  22.6 us (97%)
  between operations  0.64 us (3%)
    pallas_call x1, Pallas kernels, shards(): pl.pallas_call(functools.partial(kernel, tiles, pair, members), out_shape...  21.9 us
    pallas_call x1, Pallas kernels, shards(): pl.pallas_call(write_out, out_shape=(jax.ShapeDtypeStruct((1, rows, width...  0.7 us

profile of v1, /device:TPU:1, one launch (start us, length us, event | category | flops | bytes accessed | tf_op | source)
XLA Modules:
  0.0 23.2 jit_solution(6374463573750753826)
XLA Ops:
  0.6 21.9 %nowcast.1 = (bf16[1,64,512]{2,1,0:T(8,128)(2,1)S(1)}, f32[64,512]{1,0:T(8,128)S(1)}) custom-call(f32[1,64,512]{2,1,0:T(8,128)} %noise_hbm.1, bf16[2,6,64,512]{3,2,1,0:T(8,128)(2,1)} %obs_hbm.1, s32[64,512]{1,0:T(8,128)} %row_hbm.1, s32[64,512]{1,0:T(8,128)} %col_hbm.1, s32[4,8]{1,0:T(4,128)} %bitcast.1, f32[2,6]{1,0:T(2,128)} %ac_hbm.1, f32[6]{0:T(128)} %scale_hbm.1, ...), custom_call_target="tpu_custom_call" | custom-call | tf_op jit(solution)/shard_map/nowcast/pallas_call | solution.py:387
  22.5 0.7 %write_out.1 = (bf16[1,64,512]{2,1,0:T(8,128)(2,1)}, f32[64,512]{1,0:T(8,128)}) custom-call(bf16[1,64,512]{2,1,0:T(8,128)(2,1)S(1)} %get-tuple-element.4.fc, f32[64,512]{1,0:T(8,128)S(1)} %get-tuple-element.5.mean), custom_call_target="tpu_custom_call" | custom-call | tf_op jit(solution)/shard_map/write_out/pallas_call | solution.py:428

commit v2 on v1

--- a/solution.py
+++ b/solution.py
@@ -14,6 +14,48 @@
 PAD = 8
 F32 = jnp.float32
 BF16 = jnp.bfloat16
+PLAN = (
+    (
+        ((0, 0, 1), (0, 2, 0), (1, 0, 1), (1, 2, 0), (0, 1, 1), (1, 1, 1)),
+        (
+            (1, 0, 0, ((2, 0), (0, 1))),
+            (1, 0, 1, ((0, 1),)),
+            (3, 0, 1, ((0, 1), (1, 0))),
+            (3, 1, 0, ((1, 0),)),
+            (3, 0, 0, ((1, 0),)),
+        ),
+    ),
+    (
+        ((0, 0, 0), (1, 3, 0), (1, 0, 0), (0, 3, 0), (0, 1, 1), (1, 1, 1)),
+        (
+            (2, 0, 1, ((0, 0), (1, 1))),
+            (2, 0, 0, ((0, 0), (1, 1))),
+            (0, 1, 0, ((1, 1), (3, 0))),
+            (0, 1, 1, ((3, 0), (1, 1))),
+            (1, 1, 0, ((2, 0),)),
+        ),
+    ),
+    (
+        ((1, 1, 0), (1, 2, 1), (0, 3, 0), (1, 3, 0), (0, 2, 1), (0, 1, 0)),
+        (
+            (2, 1, 1, ((0, 0),)),
+            (0, 0, 0, ((3, 0), (2, 1))),
+            (2, 1, 0, ((0, 0), (3, 0))),
+            (0, 0, 1, ((2, 1), (3, 0))),
+            (3, 1, 1, ((1, 0),)),
+        ),
+    ),
+    (
+        ((1, 0, 0), (0, 0, 1), (1, 3, 1), (0, 3, 1), (0, 0, 0), (1, 2, 1)),
+        (
+            (3, 1, 1, ((2, 1),)),
+            (2, 0, 1, ((3, 1),)),
+            (3, 1, 0, ((2, 1), (2, 0))),
+            (1, 0, 1, ((2, 1), (2, 0), (3, 1))),
+            (1, 0, 0, ((3, 1),)),
+        ),
+    ),
+)
 
 
 def real_basis(length):
@@ -47,6 +89,25 @@
     return high, (value - high.astype(F32)).astype(BF16)
 
 
+def planned(tiles, pair, chunks):
+    chunk_count = 1 + max(send[0] for first, _ in PLAN for send in first)
+    return pair == 2 and tiles == 2 * len(PLAN) and chunks == chunk_count
+
+
+def plan_slots():
+    return 2 + max(len(relays) for _, relays in PLAN)
+
+
+def targets(t, tiles, pair, chunks):
+    near = {u for u in (t - 1, t + 1) if 0 <= u < tiles}
+    z, x = divmod(t, pair)
+    if planned(tiles, pair, chunks):
+        first, relays = PLAN[z]
+        ends = {(a, b) for _, a, b in first} | {end for relay in relays for end in relay[3]}
+        return near | {a * pair + (x ^ b) for a, b in ends}
+    return near | {u * pair + x for u in range(tiles // pair) if u != z} | ({z * pair + 1 - x} if pair > 1 else set())
+
+
 def dot(a, b):
     return jnp.dot(a, b, preferred_element_type=F32)
 
@@ -74,9 +135,9 @@
     tiles, pair, members,
     noise_hbm, obs_hbm, row_hbm, col_hbm, rain_hbm, ac_hbm, scale_hbm, ty_hbm, tx_hbm, txt_hbm, tyt_hbm, band_hbm,
     fc_out, mean,
-    noise, obs, row, col, ty, tx, txt, txtl, rows_t, band,
+    noise, obs, shift, ty, tx, txt, rows_t, band,
     xg, pad, shifted, steady, mask, spec, gain, arrived, rain, ac, scale,
-    load_sem, send_sem, cross_sem, recv_sem, halo_send, halo_recv, mem_send, mem_recv,
+    load_sem, send_sem, cross_sem, plan_sem, recv_sem, halo_send, halo_recv, mem_send, mem_recv,
 ):
     fc = fc_out.at[0]
     rows, width = noise.shape
@@ -85,45 +146,59 @@
     depth = tiles // pair
     size = chunk_of(rows)
     chunks = rows // size
+    plan = planned(tiles, pair, chunks)
     t = lax.axis_index("tile")
     m = lax.axis_index("member")
     z = t // pair
     x = t % pair
 
     sources = [
-        (noise_hbm.at[0], noise), (txt_hbm.at[0], txt), (txt_hbm.at[1], txtl),
-        (rain_hbm, rain), (ac_hbm, ac), (scale_hbm, scale), (obs_hbm, obs), (row_hbm, row), (col_hbm, col),
+        (noise_hbm.at[0], noise), (txt_hbm, txt),
+        (rain_hbm, rain), (ac_hbm, ac), (scale_hbm, scale), (obs_hbm, obs),
         (ty_hbm, ty), (band_hbm, band),
         (tyt_hbm.at[:, pl.ds(pl.multiple_of(t * rows, rows), rows), :], rows_t), (tx_hbm, tx),
     ]
     loads = [pltpu.make_async_copy(a, b, load_sem.at[i]) for i, (a, b) in enumerate(sources)]
-    for load in loads[:3]:
+    moves = [pltpu.make_async_copy(a, shift.at[i], load_sem.at[len(sources)]) for i, a in enumerate((row_hbm, col_hbm))]
+    both_moves = pltpu.make_async_copy(shift, shift, load_sem.at[len(sources)])
+    for load in loads[:2]:
         load.start()
 
     barrier = pltpu.get_barrier_semaphore()
+    ends = [targets(u, tiles, pair, chunks) for u in range(tiles)]
     greeted = 0
-    near = sorted({pair * d for d in range(1, depth)} | {1})
-    for step in [sign * d for d in near for sign in (-1, 1)]:
-        there = jnp.logical_and(t + step >= 0, t + step < tiles)
-        greeted = greeted + there.astype(jnp.int32)
-
-        @pl.when(there)
-        def _():
-            pl.semaphore_signal(barrier, inc=1, device_id={"tile": t + step}, device_id_type=pl.DeviceIdType.MESH)
+    if plan:
+        for u in range(tiles):
+            greeted = greeted + (t == u).astype(jnp.int32) * len(ends[u])
+
+            @pl.when(t == u)
+            def _():
+                for v in range(tiles):
+                    if u in ends[v]:
+                        pl.semaphore_signal(barrier, inc=1, device_id={"tile": v}, device_id_type=pl.DeviceIdType.MESH)
+    else:
+        near = sorted({pair * d for d in range(1, depth)} | {1})
+        for step in [sign * d for d in near for sign in (-1, 1)]:
+            there = jnp.logical_and(t + step >= 0, t + step < tiles)
+            greeted = greeted + there.astype(jnp.int32)
+
+            @pl.when(there)
+            def _():
+                pl.semaphore_signal(barrier, inc=1, device_id={"tile": t + step}, device_id_type=pl.DeviceIdType.MESH)
 
     for d in range(1, members):
         pl.semaphore_signal(
             barrier, inc=1, device_id={"member": (m + d) % members}, device_id_type=pl.DeviceIdType.MESH
         )
 
-    for load in loads[3:]:
+    for load in loads[2:6] + moves + loads[6:]:
         load.start()
-    for load in loads[:3]:
+    for load in loads[:2]:
         load.wait()
     own = pl.multiple_of(t * rows, rows)
     n_hi, n_lo = split(noise[...])
-    first = dot(jnp.concatenate([n_hi, n_lo], axis=0), txt[...])
-    xg[pl.ds(own, rows), :] = (first[:rows] + first[rows:] + dot(n_hi, txtl[...])).astype(BF16)
+    first = dot(jnp.concatenate([n_hi, n_lo], axis=0), txt[0])
+    xg[pl.ds(own, rows), :] = (first[:rows] + first[rows:] + dot(n_hi, txt[1])).astype(BF16)
     pl.semaphore_wait(barrier, greeted + members - 1)
 
     def part(block, c):
@@ -155,11 +230,54 @@
         def _():
             act(0)
 
-    for c in range(chunks):
-        if pair > 1:
-            across(z, c).start()
-        for d in range(depth - 1, 0, -1):
-            both_ways(d, lambda up: along(up, d, c).start())
+    def column(other):
+        return 1 - x if other else x
+
+    def message(number, block_z, block_other, c, end_z, end_other):
+        block = block_z * pair + column(block_other)
+        mine = part(block, c)
+        return pltpu.make_async_remote_copy(
+            src_ref=mine, dst_ref=mine, send_sem=plan_sem.at[0], recv_sem=plan_sem.at[number],
+            device_id={"tile": end_z * pair + column(end_other)}, device_id_type=pl.DeviceIdType.MESH,
+        )
+
+    def slot(end_z, block_z, block_other, c):
+        passed = [relay[:3] for relay in PLAN[end_z][1]]
+        key = (block_z, block_other, c)
+        return 2 + passed.index(key) if key in passed else 1
+
+    def landed(number, count):
+        bulk = xg.at[pl.ds(0, count * size), :]
+        pltpu.make_async_copy(bulk, bulk, plan_sem.at[number]).wait()
+
+    def at_level(act):
+        for k in range(depth):
+            pl.when(z == k)(functools.partial(act, k, *PLAN[k]))
+
+    def first_sends(k, first, relays):
+        for c, a, b in first:
+            message(slot(a, k, b, c), k, 0, c, a, b).start()
+
+    def pass_on(k, first, relays):
+        for i, (block_z, block_other, c, goals) in enumerate(relays):
+            landed(2 + i, 1)
+            for a, b in goals:
+                message(slot(a, block_z, block_other ^ b, c), block_z, block_other, c, a, b).start()
+
+    def last_arrivals(k, first, relays):
+        landed(1, (tiles - 1) * chunks - len(relays))
+
+    def sends_done(k, first, relays):
+        landed(0, len(first) + sum(len(relay[3]) for relay in relays))
+
+    if plan:
+        at_level(first_sends)
+    else:
+        for c in range(chunks):
+            if pair > 1:
+                across(z, c).start()
+            for d in range(depth - 1, 0, -1):
+                both_ways(d, lambda up: along(up, d, c).start())
 
     def relay(s):
         def take(up, c):
@@ -171,7 +289,7 @@
         for c in range(chunks):
             both_ways(s, lambda up: take(up, c))
 
-    for load in loads[3:7]:
+    for load in loads[2:6]:
         load.wait()
     coef = [coefficients(ac, scale, k, width) for k in range(LEVELS)]
     for g in range(rows // 16):
@@ -211,21 +329,21 @@
     def _():
         pad[:PAD, :] = jnp.zeros((PAD, width), F32)
 
-    def shift_columns():
-        lane = lax.broadcasted_iota(jnp.int32, (rows + 2 * PAD, width), 1)
-        value = pad[...]
+    def shift_columns(start, count):
+        lane = lax.broadcasted_iota(jnp.int32, (count, width), 1)
+        value = pad[start : start + count, :]
         for dx in range(-HALO, HALO + 1):
             moved = pltpu.roll(value, dx % width, 1) if dx else value
             if dx > 0:
                 moved = jnp.where(lane >= dx, moved, 0.0)
             if dx < 0:
                 moved = jnp.where(lane < width + dx, moved, 0.0)
-            shifted[dx + HALO] = moved
+            shifted[dx + HALO, start : start + count, :] = moved
 
     def gather_rows(start, stop):
         for g in range(start, stop):
             span = pl.ds(8 * g, 8)
-            code = row[span, :] * (2 * HALO + 1) + col[span, :]
+            code = shift[0, span, :] * (2 * HALO + 1) + shift[1, span, :]
             total = jnp.zeros((8, width), F32)
             for dy in range(-HALO, HALO + 1):
                 for dx in range(-HALO, HALO + 1):
@@ -236,8 +354,16 @@
                     )
             steady[span, :] = total
 
-    for s in range(1, depth):
-        relay(s)
+    groups = rows // 8
+    shift_columns(PAD, rows)
+    both_moves.wait()
+    gather_rows(1, groups - 1)
+
+    if plan:
+        at_level(pass_on)
+    else:
+        for s in range(1, depth):
+            relay(s)
 
     @pl.when(t > 0)
     def _():
@@ -247,18 +373,15 @@
     def _():
         before.wait_recv()
 
-    groups = rows // 8
-    shift_columns()
-    loads[7].wait()
-    loads[8].wait()
-    steps = max(depth - 1, 1)
-    for s in range(1, depth):
-        gather_rows(groups * (s - 1) // steps, groups * s // steps)
-    if depth == 1:
-        gather_rows(0, groups)
-    for load in loads[9:]:
+    shift_columns(0, PAD)
+    shift_columns(rows + PAD, PAD)
+    gather_rows(0, 1)
+    gather_rows(max(groups - 1, 1), groups)
+    for load in loads[6:]:
         load.wait()
-    if pair > 1:
+    if plan:
+        at_level(last_arrivals)
+    elif pair > 1:
         for zb in range(depth):
             for c in range(chunks):
                 arrival(zb * pair + 1 - x, c)
@@ -344,7 +467,7 @@
 
     sends = [
         pltpu.make_async_remote_copy(
-            src_ref=fc, dst_ref=arrived.at[d - 1], send_sem=mem_send.at[d - 1], recv_sem=mem_recv.at[d - 1],
+            src_ref=fc, dst_ref=arrived.at[d - 1], send_sem=mem_send.at[0], recv_sem=mem_recv.at[0],
             device_id={"member": (m + d) % members}, device_id_type=pl.DeviceIdType.MESH,
         )
         for d in range(1, members)
@@ -352,12 +475,15 @@
     for send in sends:
         send.start()
 
-    for c in range(chunks):
-        for d in range(1, depth):
-            both_ways(d, lambda up: along(up, d, c).wait_send())
-        if pair > 1:
-            for zb in range(depth):
-                across(zb, c).wait_send()
+    if plan:
+        at_level(sends_done)
+    else:
+        for c in range(chunks):
+            for d in range(1, depth):
+                both_ways(d, lambda up: along(up, d, c).wait_send())
+            if pair > 1:
+                for zb in range(depth):
+                    across(zb, c).wait_send()
 
     @pl.when(t < tiles - 1)
     def _():
@@ -367,13 +493,15 @@
     def _():
         before.wait_send()
 
+    everyone = pltpu.make_async_copy(arrived, arrived, mem_recv.at[0])
+    if members > 1:
+        everyone.wait()
     total = mean[...]
     for d in range(1, members):
-        sends[d - 1].wait_recv()
         total += arrived[d - 1].astype(F32)
     mean[...] = total * (1.0 / members)
-    for send in sends:
-        send.wait_send()
+    if members > 1:
+        pltpu.make_async_copy(arrived, arrived, mem_send.at[0]).wait()
 
 
 def shards(tables, tiles, members, noise, observed, row_shift, col_shift, rain_mask, autocorr, level_scale):
@@ -383,6 +511,7 @@
     depth, chunks = tiles // pair, rows // chunk_of(rows)
     any_space = pl.BlockSpec(memory_space=pl.ANY)
     dma = pltpu.SemaphoreType.DMA
+    plan = planned(tiles, pair, chunks)
     peers = max(members - 1, 1)
     fields = pl.pallas_call(
         functools.partial(kernel, tiles, pair, members),
@@ -392,12 +521,10 @@
         scratch_shapes=[
             pltpu.VMEM((rows, width), F32),
             pltpu.VMEM(observed.shape, BF16),
-            pltpu.VMEM((rows, width), jnp.int32),
-            pltpu.VMEM((rows, width), jnp.int32),
+            pltpu.VMEM((2, rows, width), jnp.int32),
             pltpu.VMEM((height, height), BF16),
             pltpu.VMEM((width, width), BF16),
-            pltpu.VMEM((width, width), BF16),
-            pltpu.VMEM((width, width), BF16),
+            pltpu.VMEM((2, width, width), BF16),
             pltpu.VMEM((2, rows, height), BF16),
             pltpu.VMEM(tables[-1].shape, BF16),
             pltpu.VMEM((height, width), BF16),
@@ -411,14 +538,14 @@
             pltpu.SMEM(rain_mask.shape[::-1], jnp.int32),
             pltpu.SMEM(autocorr.shape, F32),
             pltpu.SMEM(level_scale.shape, F32),
-            dma((13,)),
-            dma((2, depth, chunks)),
-            dma((depth, chunks)),
-            dma((tiles, chunks)),
+            dma((11,)),
+            *([dma((1,))] * 2 if plan else [dma((2, depth, chunks)), dma((depth, chunks))]),
+            dma((plan_slots(),)) if plan else dma((1,)),
+            dma((1,)) if plan else dma((tiles, chunks)),
             dma((2,)),
             dma((2,)),
-            dma((peers,)),
-            dma((peers,)),
+            dma((1,)),
+            dma((1,)),
         ],
         compiler_params=pltpu.CompilerParams(
             collective_id=0, has_side_effects=True, vmem_limit_bytes=67043328 - 4 * 64 * 1024

time: 23.4 us -> 22.8 us (0.974)
  Pallas kernels: 22.6 us -> 22 us
    pallas_call x1, Pallas kernels: 21.9 us -> 21.3 us  [shards(): pl.pallas_call(functools.partial(kernel, tiles, pair, members), out_shape...]
where the time goes in v2:
time: 22.8 us; the launch traced here: 22.7 us
  Pallas kernels  22 us (96%)
  between operations  0.64 us (3%)
    pallas_call x1, Pallas kernels, shards(): pl.pallas_call(functools.partial(kernel, tiles, pair, members), out_shape...  21.3 us
    pallas_call x1, Pallas kernels, shards(): pl.pallas_call(write_out, out_shape=(jax.ShapeDtypeStruct((1, rows, width...  0.7 us

profile of v2, /device:TPU:1, one launch (start us, length us, event | category | flops | bytes accessed | tf_op | source)
XLA Modules:
  0.0 22.7 jit_solution(17061793432914991521)
XLA Ops:
  0.6 21.3 %nowcast.1 = (bf16[1,64,512]{2,1,0:T(8,128)(2,1)S(1)}, f32[64,512]{1,0:T(8,128)S(1)}) custom-call(f32[1,64,512]{2,1,0:T(8,128)} %noise_hbm.1, bf16[2,6,64,512]{3,2,1,0:T(8,128)(2,1)} %obs_hbm.1, s32[64,512]{1,0:T(8,128)} %row_hbm.1, s32[64,512]{1,0:T(8,128)} %col_hbm.1, s32[4,8]{1,0:T(4,128)} %bitcast.1, f32[2,6]{1,0:T(2,128)} %ac_hbm.1, f32[6]{0:T(128)} %scale_hbm.1, ...), custom_call_target="tpu_custom_call" | custom-call | tf_op jit(solution)/shard_map/nowcast/pallas_call | solution.py:516
  22.0 0.7 %write_out.1 = (bf16[1,64,512]{2,1,0:T(8,128)(2,1)}, f32[64,512]{1,0:T(8,128)}) custom-call(bf16[1,64,512]{2,1,0:T(8,128)(2,1)S(1)} %get-tuple-element.4.fc, f32[64,512]{1,0:T(8,128)S(1)} %get-tuple-element.5.mean), custom_call_target="tpu_custom_call" | custom-call | tf_op jit(solution)/shard_map/write_out/pallas_call | solution.py:555

commit v3 on v2

--- a/solution.py
+++ b/solution.py
@@ -16,43 +16,45 @@
 BF16 = jnp.bfloat16
 PLAN = (
     (
-        ((0, 0, 1), (0, 2, 0), (1, 0, 1), (1, 2, 0), (0, 1, 1), (1, 1, 1)),
+        ((1, 0, 1), (1, 1, 0), (0, 0, 1), (0, 1, 0)),
         (
-            (1, 0, 0, ((2, 0), (0, 1))),
-            (1, 0, 1, ((0, 1),)),
-            (3, 0, 1, ((0, 1), (1, 0))),
-            (3, 1, 0, ((1, 0),)),
-            (3, 0, 0, ((1, 0),)),
+            (0, 1, 1, ((1, 0),)),
+            (2, 0, 1, ((0, 1), (1, 0))),
+            (2, 0, 0, ((0, 1), (1, 0))),
+            (3, 0, 0, ((0, 1),)),
         ),
     ),
     (
-        ((0, 0, 0), (1, 3, 0), (1, 0, 0), (0, 3, 0), (0, 1, 1), (1, 1, 1)),
+        ((1, 3, 0), (1, 2, 0), (0, 2, 0), (0, 1, 1), (1, 0, 0), (1, 1, 1), (0, 0, 0)),
         (
-            (2, 0, 1, ((0, 0), (1, 1))),
-            (2, 0, 0, ((0, 0), (1, 1))),
-            (0, 1, 0, ((1, 1), (3, 0))),
-            (0, 1, 1, ((3, 0), (1, 1))),
-            (1, 1, 0, ((2, 0),)),
+            (0, 0, 1, ((3, 0),)),
+            (0, 0, 0, ((1, 1), (3, 0))),
+            (1, 1, 0, ((3, 0), (0, 0))),
+            (1, 1, 1, ((0, 0), (3, 0))),
+            (0, 1, 1, ((2, 0),)),
+            (3, 0, 0, ((2, 0), (1, 1))),
+            (0, 1, 0, ((2, 0),)),
         ),
     ),
     (
-        ((1, 1, 0), (1, 2, 1), (0, 3, 0), (1, 3, 0), (0, 2, 1), (0, 1, 0)),
+        ((1, 0, 0), (1, 2, 1), (0, 2, 1), (1, 3, 0), (0, 0, 0), (0, 3, 0)),
         (
-            (2, 1, 1, ((0, 0),)),
-            (0, 0, 0, ((3, 0), (2, 1))),
-            (2, 1, 0, ((0, 0), (3, 0))),
-            (0, 0, 1, ((2, 1), (3, 0))),
-            (3, 1, 1, ((1, 0),)),
+            (2, 1, 1, ((1, 0),)),
+            (2, 1, 0, ((1, 0),)),
+            (3, 1, 1, ((0, 0), (3, 0), (1, 0))),
+            (1, 0, 0, ((2, 1), (3, 0))),
+            (3, 0, 1, ((1, 0),)),
         ),
     ),
     (
-        ((1, 0, 0), (0, 0, 1), (1, 3, 1), (0, 3, 1), (0, 0, 0), (1, 2, 1)),
+        ((0, 0, 0), (0, 3, 1), (1, 2, 1), (0, 1, 0), (1, 0, 0), (1, 2, 0)),
         (
-            (3, 1, 1, ((2, 1),)),
             (2, 0, 1, ((3, 1),)),
-            (3, 1, 0, ((2, 1), (2, 0))),
-            (1, 0, 1, ((2, 1), (2, 0), (3, 1))),
-            (1, 0, 0, ((3, 1),)),
+            (3, 1, 0, ((2, 0),)),
+            (2, 0, 0, ((3, 1),)),
+            (1, 0, 1, ((2, 1),)),
+            (0, 0, 1, ((2, 0), (3, 1))),
+            (0, 0, 0, ((3, 1), (2, 0))),
         ),
     ),
 )
@@ -247,7 +249,7 @@
         return 2 + passed.index(key) if key in passed else 1
 
     def landed(number, count):
-        bulk = xg.at[pl.ds(0, count * size), :]
+        bulk = spec.at[pl.ds(0, count * size // 2), :]
         pltpu.make_async_copy(bulk, bulk, plan_sem.at[number]).wait()
 
     def at_level(act):

time: 22.8 us -> 20.7 us (0.908)
  Pallas kernels: 22 us -> 19.9 us
    pallas_call x1, Pallas kernels: 21.3 us -> 19.2 us  [shards(): pl.pallas_call(functools.partial(kernel, tiles, pair, members), out_shape...]
where the time goes in v3:
time: 20.7 us; the launch traced here: 20.5 us
  Pallas kernels  19.9 us (96%)
  between operations  0.64 us (3%)
    pallas_call x1, Pallas kernels, shards(): pl.pallas_call(functools.partial(kernel, tiles, pair, members), out_shape...  19.2 us
    pallas_call x1, Pallas kernels, shards(): pl.pallas_call(write_out, out_shape=(jax.ShapeDtypeStruct((1, rows, width...  0.7 us

profile of v3, /device:TPU:1, one launch (start us, length us, event | category | flops | bytes accessed | tf_op | source)
XLA Modules:
  0.0 20.5 jit_solution(7347149431188752268)
XLA Ops:
  0.6 19.2 %nowcast.1 = (bf16[1,64,512]{2,1,0:T(8,128)(2,1)S(1)}, f32[64,512]{1,0:T(8,128)S(1)}) custom-call(f32[1,64,512]{2,1,0:T(8,128)} %noise_hbm.1, bf16[2,6,64,512]{3,2,1,0:T(8,128)(2,1)} %obs_hbm.1, s32[64,512]{1,0:T(8,128)} %row_hbm.1, s32[64,512]{1,0:T(8,128)} %col_hbm.1, s32[4,8]{1,0:T(4,128)} %bitcast.1, f32[2,6]{1,0:T(2,128)} %ac_hbm.1, f32[6]{0:T(128)} %scale_hbm.1, ...), custom_call_target="tpu_custom_call" | custom-call | tf_op jit(solution)/shard_map/nowcast/pallas_call | solution.py:518
  19.8 0.7 %write_out.1 = (bf16[1,64,512]{2,1,0:T(8,128)(2,1)}, f32[64,512]{1,0:T(8,128)}) custom-call(bf16[1,64,512]{2,1,0:T(8,128)(2,1)S(1)} %get-tuple-element.4.fc, f32[64,512]{1,0:T(8,128)S(1)} %get-tuple-element.5.mean), custom_call_target="tpu_custom_call" | custom-call | tf_op jit(solution)/shard_map/write_out/pallas_call | solution.py:557

commit v4 on v3

--- a/solution.py
+++ b/solution.py
@@ -138,7 +138,7 @@
     noise_hbm, obs_hbm, row_hbm, col_hbm, rain_hbm, ac_hbm, scale_hbm, ty_hbm, tx_hbm, txt_hbm, tyt_hbm, band_hbm,
     fc_out, mean,
     noise, obs, shift, ty, tx, txt, rows_t, band,
-    xg, pad, shifted, steady, mask, spec, gain, arrived, rain, ac, scale,
+    xg, pad, shifted, steady, mask, spec, gain, bands, squares, arrived, rain, ac, scale,
     load_sem, send_sem, cross_sem, plan_sem, recv_sem, halo_send, halo_recv, mem_send, mem_recv,
 ):
     fc = fc_out.at[0]
@@ -381,6 +381,16 @@
     gather_rows(max(groups - 1, 1), groups)
     for load in loads[6:]:
         load.wait()
+
+    def widen(i, carry):
+        span = pl.ds(pl.multiple_of(i * 8, 8), 8)
+        for k in range(LEVELS):
+            value = band[k, span, :].astype(F32)
+            bands[k, span, :] = value
+            squares[k, span, :] = value * value
+        return carry
+
+    lax.fori_loop(0, hy // 8 + 1, widen, 0)
     if plan:
         at_level(last_arrivals)
     elif pair > 1:
@@ -412,10 +422,8 @@
         edge = jnp.where(lane_one == 0, right[:, :128], 0.0)
         out = []
         for k in range(LEVELS):
-            w = band[k, top, :hx].astype(F32)
-            e = band[k, top, hx:].astype(F32)
-            out.append((sums[2 * k] + fold(w * w * energy)))
-            out.append((sums[2 * k + 1] + fold(e * e * edge)))
+            out.append((sums[2 * k] + fold(squares[k, top, :hx] * energy)))
+            out.append((sums[2 * k + 1] + fold(squares[k, top, hx:] * edge)))
         return tuple(out)
 
     sc, ss = spec[hy : hy + 8, :hx], spec[hy : hy + 8, hx:]
@@ -425,9 +433,7 @@
     corner = jnp.where(jnp.logical_and(first_row[:, :128], lane_one[:8] == 0), ss[:, :128], 0.0)
     sums = []
     for k in range(LEVELS):
-        w = band[k, hy:, :hx].astype(F32)
-        e = band[k, hy:, hx:].astype(F32)
-        sums += [w * w * bottom, e * e * corner]
+        sums += [squares[k, hy:, :hx] * bottom, squares[k, hy:, hx:] * corner]
     sums = lax.fori_loop(0, hy // strip, powers, tuple(sums), unroll=2)
     levels = []
     for k in range(LEVELS):
@@ -436,15 +442,15 @@
         levels.append(coef[k][2][:, :1] / jnp.sqrt(power + 1e-06))
     level = [jnp.broadcast_to(v, (1, hx + 128)) for v in levels]
 
-    last = sum(level[k] * band[k, hy:, :].astype(F32) for k in range(LEVELS))[:1]
+    last = sum(level[k] * bands[k, hy:, :] for k in range(LEVELS))[:1]
 
     def apply(i, carry):
         r = pl.multiple_of(i * strip, strip)
         top = pl.ds(r, strip)
         low = pl.ds(hy + r, strip)
-        a = level[0] * band[0, top, :].astype(F32)
+        a = level[0] * bands[0, top, :]
         for k in range(1, LEVELS):
-            a += level[k] * band[k, top, :].astype(F32)
+            a += level[k] * bands[k, top, :]
 
         def right_of(v):
             begin = jnp.where(lane_one == 0, v[:, hx:], v[:, :128])
@@ -536,6 +542,8 @@
             pltpu.VMEM((rows, width), F32),
             pltpu.VMEM((height, width), F32),
             pltpu.VMEM((height, width), BF16),
+            pltpu.VMEM(tables[-1].shape, F32),
+            pltpu.VMEM(tables[-1].shape, F32),
             pltpu.VMEM((peers, rows, width), BF16),
             pltpu.SMEM(rain_mask.shape[::-1], jnp.int32),
             pltpu.SMEM(autocorr.shape, F32),

time: 20.7 us -> 20.4 us (0.986)
  Pallas kernels: 19.9 us -> 19.6 us
    pallas_call x1, Pallas kernels: 19.2 us -> 18.9 us  [shards(): pl.pallas_call(functools.partial(kernel, tiles, pair, members), out_shape...]
where the time goes in v4:
time: 20.4 us; the launch traced here: 20.3 us
  Pallas kernels  19.6 us (96%)
  between operations  0.64 us (3%)
    pallas_call x1, Pallas kernels, shards(): pl.pallas_call(functools.partial(kernel, tiles, pair, members), out_shape...  18.9 us
    pallas_call x1, Pallas kernels, shards(): pl.pallas_call(write_out, out_shape=(jax.ShapeDtypeStruct((1, rows, width...  0.7 us

profile of v4, /device:TPU:1, one launch (start us, length us, event | category | flops | bytes accessed | tf_op | source)
XLA Modules:
  0.0 20.3 jit_solution(6764395348568232540)
XLA Ops:
  0.6 18.9 %nowcast.1 = (bf16[1,64,512]{2,1,0:T(8,128)(2,1)S(1)}, f32[64,512]{1,0:T(8,128)S(1)}) custom-call(f32[1,64,512]{2,1,0:T(8,128)} %noise_hbm.1, bf16[2,6,64,512]{3,2,1,0:T(8,128)(2,1)} %obs_hbm.1, s32[64,512]{1,0:T(8,128)} %row_hbm.1, s32[64,512]{1,0:T(8,128)} %col_hbm.1, s32[4,8]{1,0:T(4,128)} %bitcast.1, f32[2,6]{1,0:T(2,128)} %ac_hbm.1, f32[6]{0:T(128)} %scale_hbm.1, ...), custom_call_target="tpu_custom_call" | custom-call | tf_op jit(solution)/shard_map/nowcast/pallas_call | solution.py:524
  19.6 0.7 %write_out.1 = (bf16[1,64,512]{2,1,0:T(8,128)(2,1)}, f32[64,512]{1,0:T(8,128)}) custom-call(bf16[1,64,512]{2,1,0:T(8,128)(2,1)S(1)} %get-tuple-element.4.fc, f32[64,512]{1,0:T(8,128)S(1)} %get-tuple-element.5.mean), custom_call_target="tpu_custom_call" | custom-call | tf_op jit(solution)/shard_map/write_out/pallas_call | solution.py:565

commit v5 on v4

--- a/solution.py
+++ b/solution.py
@@ -16,45 +16,40 @@
 BF16 = jnp.bfloat16
 PLAN = (
     (
-        ((1, 0, 1), (1, 1, 0), (0, 0, 1), (0, 1, 0)),
+        ((0, 1, 0), (1, 3, 0), (0, 3, 0), (1, 0, 1), (0, 0, 1), (1, 1, 0), (1, 1, 1)),
         (
-            (0, 1, 1, ((1, 0),)),
-            (2, 0, 1, ((0, 1), (1, 0))),
-            (2, 0, 0, ((0, 1), (1, 0))),
-            (3, 0, 0, ((0, 1),)),
+            (2, 1, 1, ((0, 1), (1, 1))),
+            (2, 1, 0, ((0, 1), (1, 1))),
+            (3, 0, 1, ((0, 1), (1, 1))),
         ),
     ),
     (
-        ((1, 3, 0), (1, 2, 0), (0, 2, 0), (0, 1, 1), (1, 0, 0), (1, 1, 1), (0, 0, 0)),
+        ((0, 2, 1), (1, 1, 1), (0, 1, 1), (0, 3, 0), (1, 3, 0), (1, 0, 0), (0, 0, 0)),
         (
-            (0, 0, 1, ((3, 0),)),
-            (0, 0, 0, ((1, 1), (3, 0))),
-            (1, 1, 0, ((3, 0), (0, 0))),
-            (1, 1, 1, ((0, 0), (3, 0))),
-            (0, 1, 1, ((2, 0),)),
-            (3, 0, 0, ((2, 0), (1, 1))),
-            (0, 1, 0, ((2, 0),)),
+            (1, 1, 1, ((0, 0), (2, 0))),
+            (0, 0, 0, ((2, 1), (2, 0), (1, 1))),
+            (1, 1, 0, ((0, 0),)),
+            (0, 0, 1, ((2, 1), (2, 0))),
         ),
     ),
     (
-        ((1, 0, 0), (1, 2, 1), (0, 2, 1), (1, 3, 0), (0, 0, 0), (0, 3, 0)),
+        ((1, 2, 1), (0, 3, 0), (1, 0, 1), (0, 2, 1), (1, 3, 0), (0, 0, 1)),
         (
-            (2, 1, 1, ((1, 0),)),
+            (2, 1, 1, ((3, 0), (1, 0))),
             (2, 1, 0, ((1, 0),)),
-            (3, 1, 1, ((0, 0), (3, 0), (1, 0))),
-            (1, 0, 0, ((2, 1), (3, 0))),
-            (3, 0, 1, ((1, 0),)),
+            (3, 0, 1, ((2, 1), (1, 0))),
+            (3, 0, 0, ((2, 1), (1, 0))),
         ),
     ),
     (
-        ((0, 0, 0), (0, 3, 1), (1, 2, 1), (0, 1, 0), (1, 0, 0), (1, 2, 0)),
+        ((1, 0, 0), (1, 2, 0), (1, 3, 1), (0, 0, 0), (0, 3, 1), (0, 2, 0)),
         (
-            (2, 0, 1, ((3, 1),)),
-            (3, 1, 0, ((2, 0),)),
             (2, 0, 0, ((3, 1),)),
-            (1, 0, 1, ((2, 1),)),
-            (0, 0, 1, ((2, 0), (3, 1))),
-            (0, 0, 0, ((3, 1), (2, 0))),
+            (3, 1, 0, ((0, 0), (1, 0))),
+            (1, 0, 0, ((3, 1), (2, 0))),
+            (1, 0, 1, ((2, 0), (3, 1))),
+            (0, 0, 1, ((3, 1),)),
+            (0, 0, 0, ((3, 1),)),
         ),
     ),
 )

time: 20.4 us -> 20 us (0.980)
  Pallas kernels: 19.6 us -> 19.2 us
    pallas_call x1, Pallas kernels: 18.9 us -> 18.6 us  [shards(): pl.pallas_call(functools.partial(kernel, tiles, pair, members), out_shape...]
where the time goes in v5:
time: 20 us; the launch traced here: 19.9 us
  Pallas kernels  19.2 us (96%)
  between operations  0.64 us (3%)
    pallas_call x1, Pallas kernels, shards(): pl.pallas_call(functools.partial(kernel, tiles, pair, members), out_shape...  18.6 us
    pallas_call x1, Pallas kernels, shards(): pl.pallas_call(write_out, out_shape=(jax.ShapeDtypeStruct((1, rows, width...  0.7 us

profile of v5, /device:TPU:1, one launch (start us, length us, event | category | flops | bytes accessed | tf_op | source)
XLA Modules:
  0.0 19.9 jit_solution(16180666844570088286)
XLA Ops:
  0.6 18.6 %nowcast.1 = (bf16[1,64,512]{2,1,0:T(8,128)(2,1)S(1)}, f32[64,512]{1,0:T(8,128)S(1)}) custom-call(f32[1,64,512]{2,1,0:T(8,128)} %noise_hbm.1, bf16[2,6,64,512]{3,2,1,0:T(8,128)(2,1)} %obs_hbm.1, s32[64,512]{1,0:T(8,128)} %row_hbm.1, s32[64,512]{1,0:T(8,128)} %col_hbm.1, s32[4,8]{1,0:T(4,128)} %bitcast.1, f32[2,6]{1,0:T(2,128)} %ac_hbm.1, f32[6]{0:T(128)} %scale_hbm.1, ...), custom_call_target="tpu_custom_call" | custom-call | tf_op jit(solution)/shard_map/nowcast/pallas_call | solution.py:519
  19.2 0.7 %write_out.1 = (bf16[1,64,512]{2,1,0:T(8,128)(2,1)}, f32[64,512]{1,0:T(8,128)}) custom-call(bf16[1,64,512]{2,1,0:T(8,128)(2,1)S(1)} %get-tuple-element.4.fc, f32[64,512]{1,0:T(8,128)S(1)} %get-tuple-element.5.mean), custom_call_target="tpu_custom_call" | custom-call | tf_op jit(solution)/shard_map/write_out/pallas_call | solution.py:560
